TPU v7x, 32 devices: a whole 2x2x4 slice. The times are simulated.
32 devices in a mesh: dp: 16 (over z, y, x), tensor: 2 (over core).
Axes of the slice: x: 2, y: 2, z: 4, core: 2. Of those that a mesh axis runs over, the one named last changes fastest.
Arguments:
- hidden: bfloat16 [128, 4096], P('dp'), may hold values from -20 to 20
- gain: bfloat16 [4096], replicated, may hold values from 0.5 to 1.5
- head: bfloat16 [4096, 4096], P(('dp', 'tensor')), may hold values from -32 to 32
- moment: bfloat16 [4096, 4096], P(('dp', 'tensor')), may hold values from -6 to 6
- second: float32 [4096], P(('dp', 'tensor')), may hold values from 0.5 to 50
- labels: int32 [128], P('dp'), may hold values from 0 to 4095
Outputs:
- grad_hidden: bfloat16 [128, 4096], P('dp')
- grad_gain: float32 [4096], replicated
- head_new: bfloat16 [4096, 4096], P(('dp', 'tensor'))
- moment_new: bfloat16 [4096, 4096], P(('dp', 'tensor'))
- second_new: float32 [4096], P(('dp', 'tensor'))
All inputs are finite; a program needn't handle non-finite values.
Results may differ from a plain program's by a relative error of at most 0.01.
Values may be sent and summed in bfloat16 or wider, within the bound.
A program may use at most 64 MiB of HBM per device.

v0:
```python
import jax
import jax.numpy as jnp
from jax import lax
from jax.sharding import PartitionSpec as P

D = 4096


loss_scale = 16.0
beta_one = 0.9
beta_two = 0.999
adam_eps = 1e-08
step_size = 0.02
norm_eps = 1e-05
bias_one = 1.0 - 0.9**10
bias_two = 1.0 - 0.999**10


def inverse_norm(values_f):
    squares = jnp.sum(values_f * values_f, axis=1)
    return lax.rsqrt(squares / D + norm_eps)


def softmax_grad(logits, targets, vocab_ids):
    local_max = jnp.max(logits, axis=1)
    local_sum = jnp.sum(jnp.exp(logits - local_max[:, None]), axis=1)
    global_max = lax.pmax(local_max, ("dp", "tensor"))
    global_sum = lax.psum(local_sum * jnp.exp(local_max - global_max), ("dp", "tensor"))
    onehot = (targets[:, None] == vocab_ids[None, :]).astype(jnp.float32)
    probability = jnp.exp(logits - global_max[:, None]) / global_sum[:, None]
    return (loss_scale * (probability - onehot)).astype(jnp.bfloat16)


def norm_backward(grad_normed, hidden_part, rstd_part, gain_f):
    inner_sums = jnp.sum(grad_normed * gain_f * hidden_part, axis=1)
    return (
        rstd_part[:, None] * gain_f * grad_normed
        - hidden_part * (rstd_part**3)[:, None] * inner_sums[:, None] / D
    ).astype(jnp.bfloat16)


def local(hidden, gain, head, moment, second, labels):
    hidden_f = hidden.astype(jnp.float32)
    gain_f = gain.astype(jnp.float32)
    rstd = inverse_norm(hidden_f)
    normed = (hidden_f * rstd[:, None] * gain_f).astype(jnp.bfloat16)
    normed_all = lax.all_gather(normed, "dp", axis=0, tiled=True)
    all_labels = lax.all_gather(labels, "dp", axis=0, tiled=True)
    own_rows = head.shape[0]
    tensor_count = lax.axis_size("tensor")
    dp_count = lax.axis_size("dp")
    owner = lax.axis_index("dp") * tensor_count + lax.axis_index("tensor")
    vocab_ids = owner * own_rows + jnp.arange(own_rows, dtype=jnp.int32)
    logits = lax.dot_general(
        normed_all, head, (((1,), (1,)), ((), ())), preferred_element_type=jnp.float32
    )
    dlogits = softmax_grad(logits, all_labels, vocab_ids)
    grad_head = lax.dot_general(
        dlogits, normed_all, (((0,), (0,)), ((), ())), preferred_element_type=jnp.float32
    )
    share_rows = hidden.shape[0] // tensor_count
    ordered = dlogits.reshape(dp_count, tensor_count, share_rows, own_rows).transpose(1, 0, 2, 3)
    ordered = ordered.reshape(tensor_count * dp_count * share_rows, own_rows)
    tensor_sum = lax.psum_scatter(
        jnp.dot(ordered, head, preferred_element_type=jnp.float32).astype(jnp.bfloat16),
        "tensor",
        scatter_dimension=0,
        tiled=True,
    ).astype(jnp.float32)
    full_sum = lax.psum(tensor_sum, "dp")
    grad_normed = lax.dynamic_slice_in_dim(
        full_sum, lax.axis_index("dp") * share_rows, share_rows, 0
    )
    offset = lax.axis_index("tensor") * share_rows
    hidden_part = lax.dynamic_slice_in_dim(hidden_f, offset, share_rows, 0)
    rstd_part = lax.dynamic_slice_in_dim(rstd, offset, share_rows, 0)
    grad_gain = lax.psum(
        jnp.sum(grad_normed * hidden_part * rstd_part[:, None], axis=0), ("dp", "tensor")
    )
    part_grad = norm_backward(grad_normed, hidden_part, rstd_part, gain_f)
    grad_hidden = lax.all_gather(part_grad, "tensor", axis=0, tiled=True)
    row_sums = jnp.sum(grad_head * grad_head, axis=1)
    second_new = beta_two * second + (1.0 - beta_two) * row_sums / D
    first = beta_one * moment.astype(jnp.float32) + (1.0 - beta_one) * grad_head
    adam_step = first / bias_one / (jnp.sqrt(second_new / bias_two)[:, None] + adam_eps)
    head_new = (head.astype(jnp.float32) - step_size * adam_step).astype(jnp.bfloat16)
    return (grad_hidden, grad_gain, head_new, first.astype(jnp.bfloat16), second_new)


def solution(mesh):
    placed = (
        P("dp", None),
        P(),
        P(("dp", "tensor"), None),
        P(("dp", "tensor"), None),
        P(("dp", "tensor")),
        P("dp"),
    )
    return jax.shard_map(
        local,
        mesh=mesh,
        in_specs=placed,
        out_specs=(
            P("dp", None),
            P(),
            P(("dp", "tensor"), None),
            P(("dp", "tensor"), None),
            P(("dp", "tensor")),
        ),
        check_vma=False,
    )
```

profile of v0, /device:TPU:0, one launch (start us, length us, event | category | flops | bytes accessed | tf_op | source)
XLA Modules:
  0.0 298.0 jit_solution(8603135255991691037)
XLA Ops:
  7.2 0.8 convert_element_type.37
  8.0 1.0 multiply_reduce_fusion.1
  9.0 1.6 multiply_convert_fusion
  10.6 1.2 dynamic-slice
  12.5 0.9 dynamic-update-slice
  13.4 16.2 %all-reduce = s32[128]{0:T(128)S(1)} all-reduce(s32[128]{0:T(128)S(1)} %dynamic-update-slice), channel_id=1, replica_groups=mesh['dp'=16,'tensor'=2] {'dp'}, use_global_device_ids=true, to_apply=%add | all-reduce | flops 128 | bytes 1024
  29.6 39.8 %all-gather.3.cloned.1.call-done = bf16[128,4096]{1,0:T(8,128)(2,1)} async-done(((bf16[8,4096]{1,0:T(8,128)(2,1)}), bf16[128,4096]{1,0:T(8,128)(2,1)}) %all-gather.3.cloned.1.call-update) | async-done | bytes 1048592 | tf_op jit(solution)/shard_map/all_gather | solution.py:47
  69.4 2.1 fusion.2
  71.4 38.5 %pmax.7 = f32[128]{0:T(128)S(1)} all-reduce(f32[128]{0:T(128)S(1)} %get-tuple-element.13), channel_id=1, replica_groups=mesh['dp'=16,'tensor'=2] {'dp','tensor'}, use_global_device_ids=true, to_apply=%region_2.0 | all-reduce | flops 128 | bytes 1024 | tf_op jit(solution)/shard_map/pmax | solution.py:27
  109.9 0.2 exponential_reduce_fusion
  110.1 40.9 %psum.21 = f32[128]{0:T(128)S(1)} all-reduce(f32[128]{0:T(128)S(1)} %exponential_multiply_fusion), channel_id=1, replica_groups=mesh['dp'=16,'tensor'=2] {'dp','tensor'}, use_global_device_ids=true, to_apply=%region_4.0 | all-reduce | flops 128 | bytes 1024 | tf_op jit(solution)/shard_map/psum | solution.py:28
  151.0 0.1 multiply_convert_fusion.1
  151.1 1.5 convolution_convert_fusion
  152.7 0.1 multiply_multiply_fusion
  152.8 0.5 multiply_reduce_fusion
  153.3 0.5 sqrt_add_fusion
  153.8 2.1 fusion
  155.9 4.9 %reduce-scatter.2.cloned.1.call-done = bf16[64,4096]{1,0:T(8,128)(2,1)} async-done(((bf16[128,4096]{1,0:T(8,128)(2,1)}), bf16[64,4096]{1,0:T(8,128)(2,1)}) %reduce-scatter.2.cloned.1.call-update) | async-done | bytes 524304 | tf_op jit(solution)/shard_map/reduce_scatter | solution.py:64
  160.8 90.6 %all-reduce.2 = f32[64,4096]{1,0:T(8,128)S(1)} all-reduce(bf16[64,4096]{1,0:T(8,128)(2,1)} %reduce-scatter.2.cloned.1.call-done), channel_id=1, replica_groups=mesh['dp'=16,'tensor'=2] {'dp'}, use_global_device_ids=true, to_apply=%region_6.0 | all-reduce | flops 262144 | bytes 1572864 | tf_op jit(solution)/shard_map/psum | solution.py:70
  251.5 0.2 multiply_reduce_fusion.2
  251.7 0.1 fusion.1
  251.8 1.9 all-gather
  253.6 0.7 reshape.41
  254.3 36.9 %psum.23 = f32[4096]{0:T(1024)} all-reduce(f32[4096]{0:T(1024)S(1)} %get-tuple-element.5), channel_id=1, replica_groups=mesh['dp'=16,'tensor'=2] {'dp','tensor'}, use_global_device_ids=true, to_apply=%region_9.0 | all-reduce | flops 4096 | bytes 32768 | tf_op jit(solution)/shard_map/psum | solution.py:77
  (20 shorter events, 0.2 us)
Async XLA Ops:
  7.2 144.0 %copy-start = (bf16[128,4096]{1,0:T(8,128)(2,1)S(1)}, bf16[128,4096]{1,0:T(8,128)(2,1)}, u32[]{:S(2)}) copy-start(bf16[128,4096]{1,0:T(8,128)(2,1)} %param.8) | copy-start | bytes 3145732
  7.2 62.2 %all-gather.3.cloned.1.call-start = ((), (), s32[]{:S(2)}) async-start(), calls=%async_computation.1 | async-start | bytes 1114112 | tf_op jit(solution)/shard_map/all_gather | solution.py:47
  10.6 150.2 %reduce-scatter.2.cloned.1.call-start = ((), (), s32[]{:S(2)}) async-start(), calls=%async_computation.2 | async-start | bytes 1572864 | tf_op jit(solution)/shard_map/reduce_scatter | solution.py:64
  71.4 81.2 %copy-start.3 = (bf16[8,4096]{1,0:T(8,128)(2,1)S(1)}, bf16[8,4096]{1,0:T(8,128)(2,1)}, u32[]{:S(2)}) copy-start(bf16[8,4096]{1,0:T(8,128)(2,1)} %param.6) | copy-start | bytes 196612
  71.4 81.3 %copy-start.1 = (bf16[128,4096]{1,0:T(8,128)(2,1)S(1)}, bf16[128,4096]{1,0:T(8,128)(2,1)}, u32[]{:S(2)}) copy-start(bf16[128,4096]{1,0:T(8,128)(2,1)} %all-gather.3.cloned.1.call-done) | copy-start | bytes 3145732
  152.6 0.7 copy-start.4
  152.6 1.2 copy-start.2
Sparse Core Ops, SparseCore 0:
  11.3 57.9 all-gather.2
  152.8 8.0 reduce-scatter.1
where the time goes:
time: 300 us; the launch traced here: 298 us
  blocking collectives  225 us (75%)
  waiting for transfers between devices  44.7 us (15%)
  between operations  14.8 us (5%)
  other arithmetic  6.64 us (2%)
  matrix products  4.05 us (1%)
    psum x1, blocking collectives, local(): full_sum = lax.psum(tensor_sum, 'dp')  90.6 us
    psum x1, blocking collectives, softmax_grad(): lax.psum(local_sum * jnp.exp(local_max - global_max), ('dp', 'tensor'))  40.9 us
    all_gather x1, waiting for transfers between devices, local(): normed_all = lax.all_gather(normed, 'dp', axis=0, tiled=True)  39.8 us
    pmax x1, blocking collectives, softmax_grad(): global_max = lax.pmax(local_max, ('dp', 'tensor'))  38.5 us
    psum x1, blocking collectives, local(): lax.psum(jnp.sum(grad_normed * hidden_part * rstd_part[:, None], axis=0),...  36.9 us
    unnamed x1, blocking collectives  16.2 us
  transfers between devices with their start and end apart: 2, of which 2 were waited for; matrix products, arithmetic and copies ran while one was open for 2% of the time, Pallas kernels for 0%

commit v1 on v0

--- a/solution.py
+++ b/solution.py
@@ -1,7 +1,16 @@
+import functools
+
 import jax
 import jax.numpy as jnp
 from jax import lax
+from jax.experimental import pallas as pl
+from jax.experimental.pallas import tpu as pltpu
 from jax.sharding import PartitionSpec as P
+
+MESH = pl.DeviceIdType.MESH
+LANES = 128
+PLANE = 4
+CHUNK = 512
 
 D = 4096
 
@@ -87,6 +96,488 @@
     return (grad_hidden, grad_gain, head_new, first.astype(jnp.bfloat16), second_new)
 
 
+def wide(values):
+    return values.astype(jnp.float32)
+
+
+def narrow(values):
+    return values.astype(jnp.bfloat16)
+
+
+def fused_kernel(
+    layers,
+    hidden_ref,
+    gain_ref,
+    head_hbm,
+    moment_hbm,
+    second_ref,
+    labels_ref,
+    grad_hidden_ref,
+    grad_gain_ref,
+    head_out,
+    moment_out,
+    second_out,
+    gathered,
+    normed,
+    head,
+    moment,
+    gain_wide,
+    grad_head,
+    head_new,
+    moment_new,
+    stat_own,
+    stats,
+    pair_out,
+    pair_in,
+    plane_out,
+    plane_in,
+    plane_sum,
+    line_out,
+    line_in,
+    message,
+    columns_in,
+    gather_recv,
+    gather_line,
+    gather_plane,
+    gather_pair,
+    stat_send,
+    stat_recv,
+    pair_sems,
+    plane_sems,
+    line_sems,
+    message_send,
+    message_recv,
+    local_sems,
+):
+    groups = layers * PLANE
+    devices = groups * 2
+    tokens, width = normed.shape
+    own_tokens = hidden_ref.shape[0]
+    own_rows = head.shape[0]
+    half = width // 2
+    dp = lax.axis_index("dp")
+    core = lax.axis_index("tensor")
+    other = 1 - core
+    layer = lax.div(dp, PLANE)
+    spot = lax.rem(dp, PLANE)
+    me = dp * 2 + core
+    own_block = (core * PLANE + spot) * layers + layer
+
+    def at(index):
+        return (lax.div(index, 2), lax.rem(index, 2))
+
+    def partner(step):
+        return lax.rem(me + step, devices)
+
+    def block_of(index):
+        target_dp, target_core = at(index)
+        return (target_core * PLANE + lax.rem(target_dp, PLANE)) * layers + lax.div(
+            target_dp, PLANE
+        )
+
+    def remote(source, target, send_sem, recv_sem, device):
+        return pltpu.make_async_remote_copy(
+            src_ref=source,
+            dst_ref=target,
+            send_sem=send_sem,
+            recv_sem=recv_sem,
+            device_id=device,
+            device_id_type=MESH,
+        )
+
+    head_copy = pltpu.make_async_copy(head_hbm, head, local_sems.at[0])
+    head_copy.start()
+    moment_copy = pltpu.make_async_copy(moment_hbm, moment, local_sems.at[1])
+    moment_copy.start()
+
+    barrier = pltpu.get_barrier_semaphore()
+
+    def greet(step, carry):
+        pl.semaphore_signal(barrier, inc=1, device_id=at(partner(step)), device_id_type=MESH)
+        return carry
+
+    lax.fori_loop(1, devices, greet, 0)
+
+    gain_wide[...] = wide(gain_ref[...])
+    hidden_f = wide(hidden_ref[...])
+    rstd = lax.rsqrt(jnp.sum(hidden_f * hidden_f, axis=1, keepdims=True) / width + norm_eps)
+    own = narrow(hidden_f * rstd * gain_wide[...])
+    gathered[0, dp] = own[:, :half]
+    gathered[1, dp] = own[:, half:]
+    pl.semaphore_wait(barrier, devices - 1)
+
+    def shard(side, group, send_sem, device):
+        block = gathered.at[side, group]
+        return remote(block, block, send_sem, gather_recv.at[side, group], device)
+
+    def across(step):
+        return lax.rem(layer + step, layers)
+
+    def beside(step):
+        return lax.rem(spot + step, PLANE)
+
+    def line_copy(step):
+        return shard(core, dp, gather_line.at[step], (across(step) * PLANE + spot, core))
+
+    def plane_copy(row, step):
+        return shard(
+            core,
+            across(row) * PLANE + spot,
+            gather_plane.at[row, step],
+            (layer * PLANE + beside(step), core),
+        )
+
+    def pair_copy(side, row, step):
+        group = across(row) * PLANE + beside(step)
+        return shard(side, group, gather_pair.at[row, step], (dp, other))
+
+    for step in range(1, layers):
+        line_copy(step).start()
+    for step in range(1, PLANE):
+        plane_copy(0, step).start()
+    for row in range(1, layers):
+        pair_copy(core, row, 0).wait_recv()
+        for step in range(1, PLANE):
+            plane_copy(row, step).start()
+        pair_copy(core, row, 0).start()
+    for row in range(layers):
+        for step in range(1, PLANE):
+            pair_copy(core, row, step).wait_recv()
+            pair_copy(core, row, step).start()
+
+    def half_logits(side):
+        span = pl.ds(pl.multiple_of(side * half, half), half)
+        normed[:, span] = narrow(wide(gathered[side]).reshape(tokens, half))
+        return lax.dot_general(
+            head[:, span],
+            normed[:, span],
+            (((1,), (1,)), ((), ())),
+            preferred_element_type=jnp.float32,
+        )
+
+    head_copy.wait()
+    logits = half_logits(core)
+    for row in range(layers):
+        for step in range(PLANE):
+            if row + step > 0:
+                pair_copy(other, row, step).wait_recv()
+    logits = logits + half_logits(other)
+
+    lane = lax.broadcasted_iota(jnp.int32, (1, tokens), 1)
+    targets = jnp.zeros((1, tokens), jnp.int32)
+    for item in range(own_tokens):
+        targets = jnp.where(lane == dp * own_tokens + item, labels_ref[item], targets)
+    targets = jnp.where(core == 0, targets, 0)
+    local_max = jnp.max(logits, axis=0, keepdims=True)
+    local_sum = jnp.sum(jnp.exp(logits - local_max), axis=0, keepdims=True)
+    place = lax.broadcasted_iota(jnp.int32, stat_own.shape, 0)
+    packet = jnp.where(place == 0, local_max, jnp.where(place == 1, local_sum, wide(targets)))
+    stat_own[...] = packet
+    stats[me] = packet
+
+    def stat_copy(step):
+        target = partner(step)
+        return remote(
+            stat_own, stats.at[me], stat_send.at[step], stat_recv.at[me], at(target)
+        )
+
+    def stat_start(step, carry):
+        stat_copy(step).start()
+        return carry
+
+    def stat_wait(step, carry):
+        source = partner(step)
+        remote(
+            stat_own, stats.at[source], stat_send.at[step], stat_recv.at[source], at(source)
+        ).wait_recv()
+        return carry
+
+    lax.fori_loop(1, devices, stat_start, 0)
+    lax.fori_loop(1, devices, stat_wait, 0)
+
+    every = stats[...]
+    every_max = every[:, 0:1, :]
+    global_max = jnp.max(every_max, axis=0)
+    global_sum = jnp.sum(every[:, 1:2, :] * jnp.exp(every_max - global_max), axis=0)
+    all_targets = jnp.sum(every[:, 2:3, :], axis=0).astype(jnp.int32)
+    vocab = me * own_rows + lax.broadcasted_iota(jnp.int32, (own_rows, tokens), 0)
+    onehot = wide(vocab == all_targets)
+    probability = jnp.exp(logits - global_max) / global_sum
+    scaled = loss_scale * (probability - onehot)
+    by_row = narrow(scaled)
+    by_token = narrow(scaled.T)
+
+    quarter = half // PLANE
+
+    def partial(side, step):
+        start = side * half + beside(step) * quarter
+        return jnp.dot(
+            by_token,
+            head[:, pl.ds(pl.multiple_of(start, quarter), quarter)],
+            preferred_element_type=jnp.float32,
+        )
+
+    order = [*range(1, PLANE), 0]
+
+    def pair_move(step):
+        return remote(
+            pair_out.at[step],
+            pair_in.at[step],
+            pair_sems.at[0, step],
+            pair_sems.at[1, step],
+            (dp, other),
+        )
+
+    def plane_move(step):
+        return remote(
+            plane_out.at[step],
+            plane_in.at[step],
+            plane_sems.at[0, step],
+            plane_sems.at[1, step],
+            (layer * PLANE + beside(step), core),
+        )
+
+    def line_move(step):
+        return remote(
+            line_out.at[step],
+            line_in.at[step],
+            line_sems.at[0, step],
+            line_sems.at[1, step],
+            (across(step) * PLANE + spot, core),
+        )
+
+    for step in order:
+        pair_out[step] = narrow(partial(other, step))
+        pair_move(step).start()
+    for step in order:
+        mine = partial(core, step)
+        pair_move(step).wait_recv()
+        mine = mine + wide(pair_in[step])
+        if step > 0:
+            plane_out[step] = narrow(mine)
+            plane_move(step).start()
+        else:
+            plane_sum[...] = mine
+
+    squares = jnp.zeros((own_rows, 1), jnp.float32)
+    for start in range(0, width, CHUNK):
+        piece = jnp.dot(
+            by_row, normed[:, start : start + CHUNK], preferred_element_type=jnp.float32
+        )
+        grad_head[:, start : start + CHUNK] = piece
+        squares = squares + jnp.sum(piece * piece, axis=1, keepdims=True)
+    second_wide = jnp.broadcast_to(second_ref[...], (LANES, own_rows)).T
+    second_new = beta_two * second_wide + (1.0 - beta_two) * squares / width
+    second_out[...] = second_new.T[0:1, :]
+    scale = (step_size / bias_one) / (jnp.sqrt(second_new / bias_two) + adam_eps)
+    scale = scale[:, 0:1]
+    moment_copy.wait()
+
+    def adam(index, carry):
+        span = pl.ds(pl.multiple_of(index * CHUNK, CHUNK), CHUNK)
+        first = beta_one * wide(moment[:, span]) + (1.0 - beta_one) * grad_head[:, span]
+        moment_new[:, span] = narrow(first)
+        head_new[:, span] = narrow(wide(head[:, span]) - first * scale)
+        return carry
+
+    lax.fori_loop(0, width // CHUNK, adam, 0)
+    head_store = pltpu.make_async_copy(head_new, head_out, local_sems.at[2])
+    head_store.start()
+    moment_store = pltpu.make_async_copy(moment_new, moment_out, local_sems.at[3])
+    moment_store.start()
+
+    total = plane_sum[...]
+    for step in range(1, PLANE):
+        plane_move(step).wait_recv()
+        total = total + wide(plane_in[step])
+    plane_sum[...] = total
+
+    def line_span(step):
+        return pl.ds(pl.multiple_of(across(step) * LANES, LANES), LANES)
+
+    for step in range(1, layers):
+        line_out[step] = narrow(plane_sum[:, line_span(step)])
+        line_move(step).start()
+    grad_normed = plane_sum[:, line_span(0)]
+    for step in range(1, layers):
+        line_move(step).wait_recv()
+        grad_normed = grad_normed + wide(line_in[step])
+
+    own_span = pl.ds(pl.multiple_of(own_block * LANES, LANES), LANES)
+    gain_part = (
+        jnp.sum(grad_normed * wide(normed[:, own_span]), axis=0, keepdims=True)
+        / gain_wide[:, own_span]
+    )
+    gain_high = wide(narrow(gain_part))
+    gain_low = gain_part - gain_high
+    row = lax.broadcasted_iota(jnp.int32, (own_tokens, LANES), 0)
+    tail = jnp.where(row == 0, gain_high, jnp.where(row == 1, gain_low, 0.0))
+    sums = grad_normed.reshape(groups, own_tokens, LANES)
+    tails = jnp.broadcast_to(tail[None], sums.shape)
+    message[...] = narrow(jnp.concatenate([sums, tails], axis=1))
+    columns_in[own_block] = message[dp]
+
+    def message_start(step, carry):
+        target = at(partner(step))
+        remote(
+            message.at[target[0]],
+            columns_in.at[own_block],
+            message_send.at[step],
+            message_recv.at[own_block],
+            target,
+        ).start()
+        return carry
+
+    def message_wait(step, carry):
+        source = partner(step)
+        block = block_of(source)
+        remote(
+            message.at[0],
+            columns_in.at[block],
+            message_send.at[step],
+            message_recv.at[block],
+            at(source),
+        ).wait_recv()
+        return carry
+
+    lax.fori_loop(1, devices, message_start, 0)
+
+    for step in range(1, layers):
+        line_copy(step).wait_send()
+        line_move(step).wait_send()
+    for step_row in range(layers):
+        for step in range(PLANE):
+            if step > 0:
+                plane_copy(step_row, step).wait_send()
+            if step_row + step > 0:
+                pair_copy(core, step_row, step).wait_send()
+    for step in range(PLANE):
+        pair_move(step).wait_send()
+        if step > 0:
+            plane_move(step).wait_send()
+
+    def stat_done(step, carry):
+        stat_copy(step).wait_send()
+        return carry
+
+    lax.fori_loop(1, devices, stat_done, 0)
+    lax.fori_loop(1, devices, message_wait, 0)
+
+    pieces = []
+    for block in range(devices):
+        arrived = wide(columns_in[block])
+        pieces.append(arrived[:own_tokens])
+        grad_gain_ref[block : block + 1, :] = (
+            arrived[own_tokens : own_tokens + 1] + arrived[own_tokens + 1 : own_tokens + 2]
+        )
+    summed = jnp.concatenate(pieces, axis=1) * gain_wide[...]
+    inner = jnp.sum(summed * hidden_f, axis=1, keepdims=True)
+    grad_hidden_ref[...] = narrow(
+        rstd * summed - hidden_f * (rstd * rstd * rstd * inner / width)
+    )
+
+    def message_done(step, carry):
+        target = at(partner(step))
+        remote(
+            message.at[target[0]],
+            columns_in.at[own_block],
+            message_send.at[step],
+            message_recv.at[own_block],
+            target,
+        ).wait_send()
+        return carry
+
+    lax.fori_loop(1, devices, message_done, 0)
+    head_store.wait()
+    moment_store.wait()
+
+
+def fused(groups, hidden, gain, head, moment, second, labels):
+    own_tokens, width = hidden.shape
+    own_rows = head.shape[0]
+    layers = groups // PLANE
+    tokens = groups * own_tokens
+    devices = groups * 2
+    bf16, f32 = jnp.bfloat16, jnp.float32
+    quarter = width // 2 // PLANE
+    vmem = pl.BlockSpec(memory_space=pltpu.VMEM)
+    anywhere = pl.BlockSpec(memory_space=pl.ANY)
+    dma = pltpu.SemaphoreType.DMA
+    grad_hidden, grad_gain, head_new, moment_new, second_new = pl.pallas_call(
+        functools.partial(fused_kernel, layers),
+        out_shape=(
+            jax.ShapeDtypeStruct(hidden.shape, bf16),
+            jax.ShapeDtypeStruct((devices, LANES), f32),
+            jax.ShapeDtypeStruct(head.shape, bf16),
+            jax.ShapeDtypeStruct(head.shape, bf16),
+            jax.ShapeDtypeStruct((1, own_rows), f32),
+        ),
+        in_specs=[
+            vmem,
+            vmem,
+            anywhere,
+            anywhere,
+            vmem,
+            pl.BlockSpec(memory_space=pltpu.SMEM),
+        ],
+        out_specs=(vmem, vmem, anywhere, anywhere, vmem),
+        scratch_shapes=[
+            pltpu.VMEM((2, groups, own_tokens, width // 2), bf16),
+            pltpu.VMEM((tokens, width), bf16),
+            pltpu.VMEM((own_rows, width), bf16),
+            pltpu.VMEM((own_rows, width), bf16),
+            pltpu.VMEM((1, width), f32),
+            pltpu.VMEM((own_rows, width), f32),
+            pltpu.VMEM((own_rows, width), bf16),
+            pltpu.VMEM((own_rows, width), bf16),
+            pltpu.VMEM((8, tokens), f32),
+            pltpu.VMEM((devices, 8, tokens), f32),
+            pltpu.VMEM((PLANE, tokens, quarter), bf16),
+            pltpu.VMEM((PLANE, tokens, quarter), bf16),
+            pltpu.VMEM((PLANE, tokens, quarter), bf16),
+            pltpu.VMEM((PLANE, tokens, quarter), bf16),
+            pltpu.VMEM((tokens, quarter), f32),
+            pltpu.VMEM((layers, tokens, LANES), bf16),
+            pltpu.VMEM((layers, tokens, LANES), bf16),
+            pltpu.VMEM((groups, 2 * own_tokens, LANES), bf16),
+            pltpu.VMEM((devices, 2 * own_tokens, LANES), bf16),
+            dma((2, groups)),
+            dma((layers,)),
+            dma((layers, PLANE)),
+            dma((layers, PLANE)),
+            dma((devices,)),
+            dma((devices,)),
+            dma((2, PLANE)),
+            dma((2, PLANE)),
+            dma((2, layers)),
+            dma((devices,)),
+            dma((devices,)),
+            dma((4,)),
+        ],
+        compiler_params=pltpu.CompilerParams(
+            collective_id=0, has_side_effects=True, vmem_limit_bytes=40 * 1024 * 1024
+        ),
+    )(hidden, gain.reshape(1, width), head, moment, second.reshape(1, own_rows), labels)
+    return (
+        grad_hidden,
+        grad_gain.reshape(width),
+        head_new,
+        moment_new,
+        second_new.reshape(own_rows),
+    )
+
+
+def fits(mesh, hidden, head):
+    groups, cores = mesh.shape["dp"], mesh.shape["tensor"]
+    return (
+        cores == 2
+        and groups % PLANE == 0
+        and hidden.shape == (LANES, groups * cores * LANES)
+        and hidden.shape[0] == groups * 8
+        and head.shape[0] == groups * cores * LANES
+    )
+
+
 def solution(mesh):
     placed = (
         P("dp", None),
@@ -96,16 +587,23 @@
         P(("dp", "tensor")),
         P("dp"),
     )
-    return jax.shard_map(
-        local,
-        mesh=mesh,
-        in_specs=placed,
-        out_specs=(
-            P("dp", None),
-            P(),
-            P(("dp", "tensor"), None),
-            P(("dp", "tensor"), None),
-            P(("dp", "tensor")),
-        ),
-        check_vma=False,
-    )
+
+    def whole(hidden, gain, head, moment, second, labels):
+        body = local
+        if fits(mesh, hidden, head):
+            body = functools.partial(fused, mesh.shape["dp"])
+        return jax.shard_map(
+            body,
+            mesh=mesh,
+            in_specs=placed,
+            out_specs=(
+                P("dp", None),
+                P(),
+                P(("dp", "tensor"), None),
+                P(("dp", "tensor"), None),
+                P(("dp", "tensor")),
+            ),
+            check_vma=False,
+        )(hidden, gain, head, moment, second, labels)
+
+    return whole

time: 300 us -> 54.8 us (0.18)
  blocking collectives: 225 us -> 0 us
  Pallas kernels: 0 us -> 46.2 us
  waiting for transfers between devices: 44.7 us -> 0 us
  between operations: 14.8 us -> 0.69 us
  other arithmetic: 6.64 us -> 0 us
  local copies, waits for them, and re-layouts: 2.82 us -> 7.7 us
  matrix products: 4.05 us -> 0 us
    psum x3 -> x0, blocking collectives: 168 us -> none  [the longest x1 90.6 us: local(): full_sum = lax.psum(tensor_sum, 'dp')]
    pallas_call x0 -> x1, Pallas kernels: none -> 46.2 us  [fused(): pl.pallas_call(functools.partial(fused_kernel, layers), out_shape=(jax.Sh...]
    all_gather x1 -> x0, waiting for transfers between devices: 39.8 us -> none  [local(): normed_all = lax.all_gather(normed, 'dp', axis=0, tiled=True)]
    pmax x1 -> x0, blocking collectives: 38.5 us -> none  [softmax_grad(): global_max = lax.pmax(local_max, ('dp', 'tensor'))]
    unnamed x1 -> x0, blocking collectives: 16.2 us -> none
    reduce_scatter x1 -> x0, waiting for transfers between devices: 4.88 us -> none  [local(): lax.psum_scatter(jnp.dot(ordered, head, preferred_element_type=jnp.float3...]
    convert_element_type x5 -> x0, other arithmetic: 4.55 us -> none  [the longest x1 2.09 us: local(): first.astype(jnp.bfloat16)]
    unnamed x14 -> x15, local copies, waits for them, and re-layouts: 2.8 us -> 6.98 us
  transfers between devices with their start and end apart: 2 -> 0, of which waited for: 2 -> 0; matrix products, arithmetic and copies ran while one was open for 2% -> 0% of each run, Pallas kernels for 0% -> 0%
where the time goes in v1:
time: 54.8 us; the launch traced here: 54.6 us
  Pallas kernels  46.2 us (84%)
  local copies, waits for them, and re-layouts  7.7 us (14%)
  between operations  0.69 us (1%)
    pallas_call x1, Pallas kernels, fused(): pl.pallas_call(functools.partial(fused_kernel, layers), out_shape=(jax.Sh...  46.2 us
    unnamed x15, local copies, waits for them, and re-layouts  6.98 us

profile of v1, /device:TPU:0, one launch (start us, length us, event | category | flops | bytes accessed | tf_op | source)
XLA Modules:
  0.0 54.6 jit_solution(11368043611225187524)
XLA Ops:
  0.6 0.0 copy-start.3
  0.6 0.0 copy-start.4
  0.7 0.7 %reshape.22.gain_ref = bf16[1,4096]{1,0:T(2,128)(2,1)S(1)} reshape(bf16[4096]{0:T(1024)(128)(2,1)} %param.7) | data formatting | bytes 16384 | tf_op jit(solution)/shard_map/reshape | solution.py:560
  1.4 0.0 copy-done.3
  1.4 0.0 copy-done.4
  1.4 0.0 copy-start
  1.4 1.2 %copy-done = bf16[128,4096]{1,0:T(8,128)(2,1)S(1)} copy-done((bf16[128,4096]{1,0:T(8,128)(2,1)S(1)}, bf16[128,4096]{1,0:T(8,128)(2,1)}, u32[]{:S(2)}) %copy-start) | copy-done | bytes 1048600
  2.6 0.0 copy-start.1
  2.6 1.2 %copy-done.1 = bf16[128,4096]{1,0:T(8,128)(2,1)S(1)} copy-done((bf16[128,4096]{1,0:T(8,128)(2,1)S(1)}, bf16[128,4096]{1,0:T(8,128)(2,1)}, u32[]{:S(2)}) %copy-start.1) | copy-done | bytes 1048600
  3.8 0.0 copy-start.2
  3.9 0.8 %copy-done.2 = bf16[8,4096]{1,0:T(8,128)(2,1)S(1)} copy-done((bf16[8,4096]{1,0:T(8,128)(2,1)S(1)}, bf16[8,4096]{1,0:T(8,128)(2,1)}, u32[]{:S(2)}) %copy-start.2) | copy-done | bytes 65560
  4.7 46.2 %shard_map.101 = (bf16[8,4096]{1,0:T(8,128)(2,1)S(1)}, f32[32,128]{1,0:T(8,128)S(1)}, bf16[128,4096]{1,0:T(8,128)(2,1)S(1)}, bf16[128,4096]{1,0:T(8,128)(2,1)S(1)}, f32[1,128]{1,0:T(1,128)S(1)}) custom-call(bf16[8,4096]{1,0:T(8,128)(2,1)S(1)} %copy-done.2, bf16[1,4096]{1,0:T(2,128)(2,1)S(1)} %reshape.22.gain_ref, bf16[128,4096]{1,0:T(8,128)(2,1)S(1)} %copy-done, ...), custom_call_target="tpu_custom_call" | custom-call | tf_op jit(solution)/shard_map/pallas_call | solution.py:506
  50.9 0.6 %copy.16 = bf16[8,4096]{1,0:T(8,128)(2,1)} copy(bf16[8,4096]{1,0:T(8,128)(2,1)S(1)} %get-tuple-element.20) | data formatting | bytes 131072
  51.5 0.6 %copy.17 = f32[4096]{0:T(1024)} copy(f32[4096]{0:T(1024)S(1)} %bitcast.3) | data formatting | bytes 32768
  52.1 1.0 %copy.18 = bf16[128,4096]{1,0:T(8,128)(2,1)} copy(bf16[128,4096]{1,0:T(8,128)(2,1)S(1)} %get-tuple-element.22) | data formatting | bytes 2097152
  53.1 1.0 %copy.19 = bf16[128,4096]{1,0:T(8,128)(2,1)} copy(bf16[128,4096]{1,0:T(8,128)(2,1)S(1)} %get-tuple-element.23) | data formatting | bytes 2097152
  54.0 0.5 copy.20
Async XLA Ops:
  0.6 0.7 %copy-start.3 = (f32[128]{0:T(128)S(1)}, f32[128]{0:T(128)}, u32[]{:S(2)}) copy-start(f32[128]{0:T(128)} %param.10) | copy-start | bytes 1540
  0.6 0.7 %copy-start.4 = (s32[8]{0:T(128)S(1)}, s32[8]{0:T(128)}, u32[]{:S(2)}) copy-start(s32[8]{0:T(128)} %labels_ref.1) | copy-start | bytes 100
  1.4 1.2 %copy-start = (bf16[128,4096]{1,0:T(8,128)(2,1)S(1)}, bf16[128,4096]{1,0:T(8,128)(2,1)}, u32[]{:S(2)}) copy-start(bf16[128,4096]{1,0:T(8,128)(2,1)} %head_hbm.1) | copy-start | bytes 3145732
  2.6 1.2 %copy-start.1 = (bf16[128,4096]{1,0:T(8,128)(2,1)S(1)}, bf16[128,4096]{1,0:T(8,128)(2,1)}, u32[]{:S(2)}) copy-start(bf16[128,4096]{1,0:T(8,128)(2,1)} %moment_hbm.1) | copy-start | bytes 3145732
  3.8 0.8 %copy-start.2 = (bf16[8,4096]{1,0:T(8,128)(2,1)S(1)}, bf16[8,4096]{1,0:T(8,128)(2,1)}, u32[]{:S(2)}) copy-start(bf16[8,4096]{1,0:T(8,128)(2,1)} %hidden_ref.1) | copy-start | bytes 196612

commit v2 on v1

v2 whole, which is shorter than its diff:
```python
import functools

import jax
import jax.numpy as jnp
from jax import lax
from jax.experimental import pallas as pl
from jax.experimental.pallas import tpu as pltpu
from jax.sharding import PartitionSpec as P

MESH = pl.DeviceIdType.MESH
LANES = 128
PLANE = 4
CHUNK = 512
VMEM_BYTES = 61440 * 1024

D = 4096


loss_scale = 16.0
beta_one = 0.9
beta_two = 0.999
adam_eps = 1e-08
step_size = 0.02
norm_eps = 1e-05
bias_one = 1.0 - 0.9**10
bias_two = 1.0 - 0.999**10


def inverse_norm(values_f):
    squares = jnp.sum(values_f * values_f, axis=1)
    return lax.rsqrt(squares / D + norm_eps)


def softmax_grad(logits, targets, vocab_ids):
    local_max = jnp.max(logits, axis=1)
    local_sum = jnp.sum(jnp.exp(logits - local_max[:, None]), axis=1)
    global_max = lax.pmax(local_max, ("dp", "tensor"))
    global_sum = lax.psum(local_sum * jnp.exp(local_max - global_max), ("dp", "tensor"))
    onehot = (targets[:, None] == vocab_ids[None, :]).astype(jnp.float32)
    probability = jnp.exp(logits - global_max[:, None]) / global_sum[:, None]
    return (loss_scale * (probability - onehot)).astype(jnp.bfloat16)


def norm_backward(grad_normed, hidden_part, rstd_part, gain_f):
    inner_sums = jnp.sum(grad_normed * gain_f * hidden_part, axis=1)
    return (
        rstd_part[:, None] * gain_f * grad_normed
        - hidden_part * (rstd_part**3)[:, None] * inner_sums[:, None] / D
    ).astype(jnp.bfloat16)


def local(hidden, gain, head, moment, second, labels):
    hidden_f = hidden.astype(jnp.float32)
    gain_f = gain.astype(jnp.float32)
    rstd = inverse_norm(hidden_f)
    normed = (hidden_f * rstd[:, None] * gain_f).astype(jnp.bfloat16)
    normed_all = lax.all_gather(normed, "dp", axis=0, tiled=True)
    all_labels = lax.all_gather(labels, "dp", axis=0, tiled=True)
    own_rows = head.shape[0]
    tensor_count = lax.axis_size("tensor")
    dp_count = lax.axis_size("dp")
    owner = lax.axis_index("dp") * tensor_count + lax.axis_index("tensor")
    vocab_ids = owner * own_rows + jnp.arange(own_rows, dtype=jnp.int32)
    logits = lax.dot_general(
        normed_all, head, (((1,), (1,)), ((), ())), preferred_element_type=jnp.float32
    )
    dlogits = softmax_grad(logits, all_labels, vocab_ids)
    grad_head = lax.dot_general(
        dlogits, normed_all, (((0,), (0,)), ((), ())), preferred_element_type=jnp.float32
    )
    share_rows = hidden.shape[0] // tensor_count
    ordered = dlogits.reshape(dp_count, tensor_count, share_rows, own_rows).transpose(1, 0, 2, 3)
    ordered = ordered.reshape(tensor_count * dp_count * share_rows, own_rows)
    tensor_sum = lax.psum_scatter(
        jnp.dot(ordered, head, preferred_element_type=jnp.float32).astype(jnp.bfloat16),
        "tensor",
        scatter_dimension=0,
        tiled=True,
    ).astype(jnp.float32)
    full_sum = lax.psum(tensor_sum, "dp")
    grad_normed = lax.dynamic_slice_in_dim(
        full_sum, lax.axis_index("dp") * share_rows, share_rows, 0
    )
    offset = lax.axis_index("tensor") * share_rows
    hidden_part = lax.dynamic_slice_in_dim(hidden_f, offset, share_rows, 0)
    rstd_part = lax.dynamic_slice_in_dim(rstd, offset, share_rows, 0)
    grad_gain = lax.psum(
        jnp.sum(grad_normed * hidden_part * rstd_part[:, None], axis=0), ("dp", "tensor")
    )
    part_grad = norm_backward(grad_normed, hidden_part, rstd_part, gain_f)
    grad_hidden = lax.all_gather(part_grad, "tensor", axis=0, tiled=True)
    row_sums = jnp.sum(grad_head * grad_head, axis=1)
    second_new = beta_two * second + (1.0 - beta_two) * row_sums / D
    first = beta_one * moment.astype(jnp.float32) + (1.0 - beta_one) * grad_head
    adam_step = first / bias_one / (jnp.sqrt(second_new / bias_two)[:, None] + adam_eps)
    head_new = (head.astype(jnp.float32) - step_size * adam_step).astype(jnp.bfloat16)
    return (grad_hidden, grad_gain, head_new, first.astype(jnp.bfloat16), second_new)


def wide(values):
    return values.astype(jnp.float32)


def narrow(values):
    return values.astype(jnp.bfloat16)


def fused_kernel(
    layers,
    hidden_hbm,
    gain_hbm,
    head_hbm,
    moment_hbm,
    second_ref,
    labels_ref,
    grad_hidden_ref,
    grad_gain_ref,
    head_out,
    moment_out,
    second_out,
    gathered,
    normed,
    hidden,
    gain,
    head,
    moment,
    gain_wide,
    grad_head,
    head_new,
    moment_new,
    stat_out,
    stat_near,
    stat_far,
    pair_out,
    pair_in,
    plane_out,
    plane_in,
    plane_sum,
    line_out,
    line_in,
    message,
    columns_in,
    gather_recv,
    gather_line,
    gather_plane,
    gather_pair,
    near_sems,
    far_sems,
    pair_sems,
    plane_sems,
    line_sems,
    message_send,
    message_recv,
    local_sems,
):
    groups = layers * PLANE
    tokens, width = normed.shape
    own_tokens = hidden.shape[0]
    own_rows = head.shape[0]
    half = width // 2
    quarter = half // PLANE
    piece_cols = quarter // 2
    layer_tokens = PLANE * own_tokens
    dp = lax.axis_index("dp")
    core = lax.axis_index("tensor")
    other = 1 - core
    layer = lax.div(dp, PLANE)
    spot = lax.rem(dp, PLANE)
    me = dp * 2 + core

    def across(step):
        return lax.rem(layer + step, layers)

    def beside(step):
        down = lax.rem(lax.div(spot, 2) + step // 2, 2)
        return down * 2 + lax.rem(lax.rem(spot, 2) + step % 2, 2)

    def far(step):
        return (across(step) * PLANE + spot, core)

    def near(step, flip=0):
        return (layer * PLANE + beside(step), lax.rem(core + flip, 2))

    near_steps = [(step, flip) for step in (3, 1, 2, 0) for flip in (0, 1) if step + flip]

    def remote(source, target, send_sem, recv_sem, device):
        return pltpu.make_async_remote_copy(
            src_ref=source,
            dst_ref=target,
            send_sem=send_sem,
            recv_sem=recv_sem,
            device_id=device,
            device_id_type=MESH,
        )

    loads = [
        pltpu.make_async_copy(source, target, local_sems.at[index])
        for index, (source, target) in enumerate(
            [(hidden_hbm, hidden), (gain_hbm, gain), (head_hbm, head), (moment_hbm, moment)]
        )
    ]
    for load in loads:
        load.start()

    barrier = pltpu.get_barrier_semaphore()
    for step, flip in near_steps:
        pl.semaphore_signal(barrier, inc=1, device_id=near(step, flip), device_id_type=MESH)
    for step in range(1, layers):
        pl.semaphore_signal(barrier, inc=1, device_id=far(step), device_id_type=MESH)

    loads[0].wait()
    loads[1].wait()
    gain_rows = wide(gain[...])
    for piece in range(width // LANES):
        gain_wide[:, piece * LANES : (piece + 1) * LANES] = gain_rows[piece : piece + 1]
    hidden_f = wide(hidden[...])
    rstd = lax.rsqrt(jnp.sum(hidden_f * hidden_f, axis=1, keepdims=True) / width + norm_eps)
    own = narrow(hidden_f * rstd * gain_wide[...])
    gathered[0, dp] = own[:, :half]
    gathered[1, dp] = own[:, half:]
    pl.semaphore_wait(barrier, len(near_steps) + layers - 1)

    def shard(side, group, send_sem, device):
        block = gathered.at[side, group]
        return remote(block, block, send_sem, gather_recv.at[side, group], device)

    def line_copy(step):
        return shard(core, dp, gather_line.at[step], far(step))

    def plane_copy(row, step):
        return shard(
            core,
            across(row) * PLANE + spot,
            gather_plane.at[row, step],
            near(step),
        )

    def pair_copy(side, row, step):
        group = across(row) * PLANE + beside(step)
        return shard(side, group, gather_pair.at[row, step], (dp, other))

    for step in range(1, layers):
        line_copy(step).start()
    for step in (3, 1, 2):
        plane_copy(0, step).start()
    for row in range(1, layers):
        pair_copy(core, row, 0).wait_recv()
        for step in (3, 1, 2):
            plane_copy(row, step).start()
        pair_copy(core, row, 0).start()
    for row in range(layers):
        for step in range(1, PLANE):
            pair_copy(core, row, step).wait_recv()
            pair_copy(core, row, step).start()

    def half_logits(side):
        span = pl.ds(pl.multiple_of(side * half, half), half)
        normed[:, span] = narrow(wide(gathered[side]).reshape(tokens, half))
        return lax.dot_general(
            head[:, span],
            normed[:, span],
            (((1,), (1,)), ((), ())),
            preferred_element_type=jnp.float32,
        )

    loads[2].wait()
    logits = half_logits(core)
    for row in range(layers):
        for step in range(PLANE):
            if row + step > 0:
                pair_copy(other, row, step).wait_recv()
    logits = logits + half_logits(other)

    lane = lax.broadcasted_iota(jnp.int32, (1, tokens), 1)
    targets = jnp.zeros((1, tokens), jnp.int32)
    for item in range(own_tokens):
        targets = jnp.where(lane == dp * own_tokens + item, labels_ref[item], targets)
    targets = jnp.where(core == 0, targets, 0)
    local_max = jnp.max(logits, axis=0, keepdims=True)
    local_sum = jnp.sum(jnp.exp(logits - local_max), axis=0, keepdims=True)
    place = lax.broadcasted_iota(jnp.int32, (8, tokens), 0)

    def packet(peak, total, ids):
        return jnp.where(place == 0, peak, jnp.where(place == 1, total, ids))

    def merge(packets):
        peak = packets[0][0:1]
        for item in packets[1:]:
            peak = jnp.maximum(peak, item[0:1])
        total = sum(item[1:2] * jnp.exp(item[0:1] - peak) for item in packets)
        return peak, total, sum(item[2:3] for item in packets)

    def near_move(step, flip):
        slot = step * 2 + flip
        return remote(
            stat_out.at[0],
            stat_near.at[slot],
            near_sems.at[0, slot],
            near_sems.at[1, slot],
            near(step, flip),
        )

    def far_move(step):
        return remote(
            stat_out.at[1], stat_far.at[step], far_sems.at[0, step], far_sems.at[1, step], far(step)
        )

    packets = [packet(local_max, local_sum, wide(targets))]
    stat_out[0] = packets[0]
    for step, flip in near_steps:
        near_move(step, flip).start()
    for step, flip in near_steps:
        near_move(step, flip).wait_recv()
        packets.append(stat_near[step * 2 + flip])
    packets = [packet(*merge(packets))]
    stat_out[1] = packets[0]
    for step in range(1, layers):
        far_move(step).start()
    for step in range(1, layers):
        far_move(step).wait_recv()
        packets.append(stat_far[step])
    global_max, global_sum, target_sum = merge(packets)
    all_targets = target_sum.astype(jnp.int32)
    vocab = me * own_rows + lax.broadcasted_iota(jnp.int32, (own_rows, tokens), 0)
    onehot = wide(vocab == all_targets)
    probability = jnp.exp(logits - global_max) / global_sum
    scaled = loss_scale * (probability - onehot)
    by_row = narrow(scaled)
    by_token = narrow(scaled.T)

    def partial(side, step):
        start = side * half + beside(step) * quarter
        return jnp.dot(
            by_token,
            head[:, pl.ds(pl.multiple_of(start, quarter), quarter)],
            preferred_element_type=jnp.float32,
        )

    order = [3, 1, 2, 0]

    def pair_move(step):
        return remote(
            pair_out.at[step],
            pair_in.at[step],
            pair_sems.at[0, step],
            pair_sems.at[1, step],
            (dp, other),
        )

    def plane_move(step, side):
        return remote(
            plane_out.at[step, side],
            plane_in.at[step, side],
            plane_sems.at[0, step, side],
            plane_sems.at[1, step, side],
            near(step),
        )

    def line_move(step, side):
        return remote(
            line_out.at[step, side],
            line_in.at[step, side],
            line_sems.at[0, step, side],
            line_sems.at[1, step, side],
            far(step),
        )

    for step in order:
        pair_out[step] = narrow(partial(other, step))
        pair_move(step).start()
    for step in order:
        mine = partial(core, step)
        pair_move(step).wait_recv()
        mine = mine + wide(pair_in[step])
        for side in range(2):
            part = mine[:, side * piece_cols : (side + 1) * piece_cols]
            if step > 0:
                plane_out[step, side] = narrow(part)
                plane_move(step, side).start()
            else:
                plane_sum[side] = part

    squares = jnp.zeros((own_rows, 1), jnp.float32)
    for start in range(0, width, CHUNK):
        piece = jnp.dot(
            by_row, normed[:, start : start + CHUNK], preferred_element_type=jnp.float32
        )
        grad_head[:, start : start + CHUNK] = piece
        squares = squares + jnp.sum(piece * piece, axis=1, keepdims=True)
    second_wide = jnp.broadcast_to(second_ref[...], (LANES, own_rows)).T
    second_new = beta_two * second_wide + (1.0 - beta_two) * squares / width
    second_out[...] = second_new.T[0:1, :]
    scale = (step_size / bias_one) / (jnp.sqrt(second_new / bias_two) + adam_eps)
    scale = scale[:, 0:1]
    loads[3].wait()

    def adam(index, carry):
        span = pl.ds(pl.multiple_of(index * CHUNK, CHUNK), CHUNK)
        first = beta_one * wide(moment[:, span]) + (1.0 - beta_one) * grad_head[:, span]
        moment_new[:, span] = narrow(first)
        head_new[:, span] = narrow(wide(head[:, span]) - first * scale)
        return carry

    lax.fori_loop(0, width // CHUNK, adam, 0)
    stores = [
        pltpu.make_async_copy(head_new, head_out, local_sems.at[4]),
        pltpu.make_async_copy(moment_new, moment_out, local_sems.at[5]),
    ]
    for store in stores:
        store.start()

    def tail_rows(values, rows):
        high = wide(narrow(values))
        row = lax.broadcasted_iota(jnp.int32, (rows, values.shape[1]), 0)
        return jnp.where(row == 0, high, jnp.where(row == 1, values - high, 0.0))

    def layer_rows(step):
        start = across(step) * layer_tokens
        return pl.ds(pl.multiple_of(start, layer_tokens), layer_tokens)

    gain_parts = []
    for side in range(2):
        total = plane_sum[side]
        for step in (3, 1, 2):
            plane_move(step, side).wait_recv()
            total = total + wide(plane_in[step, side])
        plane_sum[side] = total
        for step in range(1, layers):
            line_out[step, side, :layer_tokens] = narrow(plane_sum[side, layer_rows(step), :])
        start = core * half + spot * quarter + side * piece_cols
        span = pl.ds(pl.multiple_of(start, piece_cols), piece_cols)
        gain_part = jnp.sum(total * wide(normed[:, span]), axis=0, keepdims=True)
        gain_part = gain_part / gain_wide[:, span]
        gain_parts.append(gain_part)
        tail = narrow(tail_rows(gain_part, 16))
        for step in range(1, layers):
            line_out[step, side, layer_tokens:] = tail
            line_move(step, side).start()

    sums, gains = [], []
    for side in range(2):
        part = plane_sum[side, layer_rows(0), :]
        gain_part = gain_parts[side]
        for step in range(1, layers):
            line_move(step, side).wait_recv()
            arrived = wide(line_in[step, side])
            part = part + arrived[:layer_tokens]
            gain_part = (
                gain_part
                + arrived[layer_tokens : layer_tokens + 1]
                + arrived[layer_tokens + 1 : layer_tokens + 2]
            )
        sums.append(part)
        gains.append(gain_part)
    sums = jnp.concatenate(sums, axis=1).reshape(PLANE, own_tokens, quarter)
    tail = tail_rows(jnp.concatenate(gains, axis=1), own_tokens)
    tail = jnp.broadcast_to(tail[None], sums.shape)
    message[...] = narrow(jnp.concatenate([sums, tail], axis=1))
    own_block = core * PLANE + spot

    def message_move(step, flip, block):
        slot = step * 2 + flip
        return remote(
            message.at[beside(step)],
            columns_in.at[block],
            message_send.at[slot],
            message_recv.at[block],
            near(step, flip),
        )

    for step, flip in near_steps:
        message_move(step, flip, own_block).start()
    columns_in[own_block] = message[spot]

    for step in range(1, layers):
        line_copy(step).wait_send()
        far_move(step).wait_send()
        for side in range(2):
            line_move(step, side).wait_send()
    for row in range(layers):
        for step in range(PLANE):
            if step > 0:
                plane_copy(row, step).wait_send()
            if row + step > 0:
                pair_copy(core, row, step).wait_send()
    for step in range(PLANE):
        pair_move(step).wait_send()
        if step > 0:
            for side in range(2):
                plane_move(step, side).wait_send()
    for step, flip in near_steps:
        near_move(step, flip).wait_send()
    for step, flip in near_steps:
        source = lax.rem(core + flip, 2) * PLANE + beside(step)
        message_move(step, flip, source).wait_recv()

    pieces = []
    lines = quarter // LANES
    for block in range(2 * PLANE):
        arrived = wide(columns_in[block])
        pieces.append(arrived[:own_tokens])
        gain_row = (
            arrived[own_tokens : own_tokens + 1] + arrived[own_tokens + 1 : own_tokens + 2]
        )
        for line in range(lines):
            place = block * lines + line
            grad_gain_ref[place : place + 1, :] = gain_row[:, line * LANES : (line + 1) * LANES]
    summed = jnp.concatenate(pieces, axis=1) * gain_wide[...]
    inner = jnp.sum(summed * hidden_f, axis=1, keepdims=True)
    grad_hidden_ref[...] = narrow(
        rstd * summed - hidden_f * (rstd * rstd * rstd * inner / width)
    )
    for step, flip in near_steps:
        message_move(step, flip, own_block).wait_send()
    for store in stores:
        store.wait()


def fused(groups, hidden, gain, head, moment, second, labels):
    own_tokens, width = hidden.shape
    own_rows = head.shape[0]
    layers = groups // PLANE
    tokens = groups * own_tokens
    devices = groups * 2
    bf16, f32 = jnp.bfloat16, jnp.float32
    quarter = width // 2 // PLANE
    vmem = pl.BlockSpec(memory_space=pltpu.VMEM)
    hbm = pl.BlockSpec(memory_space=pltpu.HBM)
    dma = pltpu.SemaphoreType.DMA
    grad_hidden, grad_gain, head_new, moment_new, second_new = pl.pallas_call(
        functools.partial(fused_kernel, layers),
        out_shape=(
            jax.ShapeDtypeStruct(hidden.shape, bf16),
            jax.ShapeDtypeStruct((devices, LANES), f32),
            jax.ShapeDtypeStruct(head.shape, bf16),
            jax.ShapeDtypeStruct(head.shape, bf16),
            jax.ShapeDtypeStruct((1, own_rows), f32),
        ),
        in_specs=[hbm, hbm, hbm, hbm, vmem, pl.BlockSpec(memory_space=pltpu.SMEM)],
        out_specs=(vmem, vmem, hbm, hbm, vmem),
        scratch_shapes=[
            pltpu.VMEM((2, groups, own_tokens, width // 2), bf16),
            pltpu.VMEM((tokens, width), bf16),
            pltpu.VMEM(hidden.shape, bf16),
            pltpu.VMEM((width // LANES, LANES), bf16),
            pltpu.VMEM((own_rows, width), bf16),
            pltpu.VMEM((own_rows, width), bf16),
            pltpu.VMEM((1, width), f32),
            pltpu.VMEM((own_rows, width), f32),
            pltpu.VMEM((own_rows, width), bf16),
            pltpu.VMEM((own_rows, width), bf16),
            pltpu.VMEM((2, 8, tokens), f32),
            pltpu.VMEM((2 * PLANE, 8, tokens), f32),
            pltpu.VMEM((layers, 8, tokens), f32),
            pltpu.VMEM((PLANE, tokens, quarter), bf16),
            pltpu.VMEM((PLANE, tokens, quarter), bf16),
            pltpu.VMEM((PLANE, 2, tokens, quarter // 2), bf16),
            pltpu.VMEM((PLANE, 2, tokens, quarter // 2), bf16),
            pltpu.VMEM((2, tokens, quarter // 2), f32),
            pltpu.VMEM((layers, 2, PLANE * own_tokens + 16, quarter // 2), bf16),
            pltpu.VMEM((layers, 2, PLANE * own_tokens + 16, quarter // 2), bf16),
            pltpu.VMEM((PLANE, 2 * own_tokens, quarter), bf16),
            pltpu.VMEM((2 * PLANE, 2 * own_tokens, quarter), bf16),
            dma((2, groups)),
            dma((layers,)),
            dma((layers, PLANE)),
            dma((layers, PLANE)),
            dma((2, 2 * PLANE)),
            dma((2, layers)),
            dma((2, PLANE)),
            dma((2, PLANE, 2)),
            dma((2, layers, 2)),
            dma((2 * PLANE,)),
            dma((2 * PLANE,)),
            dma((6,)),
        ],
        compiler_params=pltpu.CompilerParams(
            collective_id=0, has_side_effects=True, vmem_limit_bytes=VMEM_BYTES
        ),
    )(hidden, gain.reshape(width // LANES, LANES), head, moment, second.reshape(1, own_rows), labels)
    return settle(grad_hidden, grad_gain, head_new, moment_new, second_new)


def settle_kernel(count, *refs):
    held, sems = refs[2 * count : -1], refs[-1]
    loads = [
        pltpu.make_async_copy(refs[i], held[i], sems.at[0, i]) for i in range(count)
    ]
    stores = [
        pltpu.make_async_copy(held[i], refs[count + i], sems.at[1, i]) for i in range(count)
    ]
    for load in loads:
        load.start()
    for load, store in zip(loads, stores):
        load.wait()
        store.start()
    for store in stores:
        store.wait()


def settle(*results):
    hbm = pl.BlockSpec(memory_space=pltpu.HBM)
    count = len(results)
    settled = pl.pallas_call(
        functools.partial(settle_kernel, count),
        out_shape=tuple(jax.ShapeDtypeStruct(x.shape, x.dtype) for x in results),
        in_specs=[hbm] * count,
        out_specs=(hbm,) * count,
        scratch_shapes=[pltpu.VMEM(x.shape, x.dtype) for x in results]
        + [pltpu.SemaphoreType.DMA((2, count))],
        compiler_params=pltpu.CompilerParams(vmem_limit_bytes=VMEM_BYTES),
    )(*results)
    grad_hidden, grad_gain, head_new, moment_new, second_new = settled
    return grad_hidden, grad_gain.reshape(-1), head_new, moment_new, second_new.reshape(-1)


def fits(mesh, hidden, head):
    groups, cores = mesh.shape["dp"], mesh.shape["tensor"]
    return (
        cores == 2
        and groups % PLANE == 0
        and hidden.shape[0] == LANES
        and hidden.shape[1] % (groups * cores * LANES) == 0
        and hidden.shape[0] == groups * 8
        and head.shape[0] == groups * cores * LANES
    )


def solution(mesh):
    placed = (
        P("dp", None),
        P(),
        P(("dp", "tensor"), None),
        P(("dp", "tensor"), None),
        P(("dp", "tensor")),
        P("dp"),
    )

    def whole(hidden, gain, head, moment, second, labels):
        body = local
        if fits(mesh, hidden, head):
            body = functools.partial(fused, mesh.shape["dp"])
        return jax.shard_map(
            body,
            mesh=mesh,
            in_specs=placed,
            out_specs=(
                P("dp", None),
                P(),
                P(("dp", "tensor"), None),
                P(("dp", "tensor"), None),
                P(("dp", "tensor")),
            ),
            check_vma=False,
        )(hidden, gain, head, moment, second, labels)

    return whole
```

time: 54.8 us -> 46.6 us (0.85)
  local copies, waits for them, and re-layouts: 7.7 us -> 0 us
    unnamed x15 -> x0, local copies, waits for them, and re-layouts: 6.98 us -> none
    pallas_call x1, Pallas kernels: 46.2 us -> 43.1 us  [fused(): pl.pallas_call(functools.partial(fused_kernel, layers), out_shape=(jax.Sh...]
    pallas_call x0 -> x1, Pallas kernels: none -> 2.69 us  [settle(): pl.pallas_call(functools.partial(settle_kernel, count), out_shape=tuple((...]
    reshape x1 -> x0, local copies, waits for them, and re-layouts: 0.72 us -> none  [fused(): gain.reshape(1, width)]
where the time goes in v2:
time: 46.6 us; the launch traced here: 46.4 us
  Pallas kernels  45.8 us (98%)
  between operations  0.64 us (1%)
    pallas_call x1, Pallas kernels, fused(): pl.pallas_call(functools.partial(fused_kernel, layers), out_shape=(jax.Sh...  43.1 us
    pallas_call x1, Pallas kernels, settle(): pl.pallas_call(functools.partial(settle_kernel, count), out_shape=tuple((...  2.69 us

profile of v2, /device:TPU:0, one launch (start us, length us, event | category | flops | bytes accessed | tf_op | source)
XLA Modules:
  0.0 46.4 jit_solution(16676969483702902371)
XLA Ops:
  0.6 43.1 %shard_map.101 = (bf16[8,4096]{1,0:T(8,128)(2,1)}, f32[32,128]{1,0:T(8,128)}, bf16[128,4096]{1,0:T(8,128)(2,1)}, bf16[128,4096]{1,0:T(8,128)(2,1)}, f32[1,128]{1,0:T(1,128)}) custom-call(bf16[8,4096]{1,0:T(8,128)(2,1)} %hidden_hbm.1, bf16[32,128]{1,0:T(8,128)(2,1)} %bitcast.4, bf16[128,4096]{1,0:T(8,128)(2,1)} %head_hbm.1, bf16[128,4096]{1,0:T(8,128)(2,1)} %moment_hbm.1, ...), custom_call_target="tpu_custom_call" | custom-call | tf_op jit(solution)/shard_map/pallas_call | solution.py:530
  43.7 2.7 %shard_map.102 = (bf16[8,4096]{1,0:T(8,128)(2,1)}, f32[32,128]{1,0:T(8,128)}, bf16[128,4096]{1,0:T(8,128)(2,1)}, bf16[128,4096]{1,0:T(8,128)(2,1)}, f32[1,128]{1,0:T(1,128)}) custom-call(bf16[8,4096]{1,0:T(8,128)(2,1)} %get-tuple-element.15.refs_0_, f32[32,128]{1,0:T(8,128)} %get-tuple-element.16.refs_1_, bf16[128,4096]{1,0:T(8,128)(2,1)} %get-tuple-element.17.refs_2_, ...), custom_call_target="tpu_custom_call" | custom-call | tf_op jit(solution)/shard_map/pallas_call | solution.py:604

commit v3 on v2

--- a/solution.py
+++ b/solution.py
@@ -12,6 +12,7 @@
 PLANE = 4
 CHUNK = 512
 VMEM_BYTES = 61440 * 1024
+SETTLE_PARTS = 4
 
 D = 4096
 
@@ -239,6 +240,15 @@
         group = across(row) * PLANE + beside(step)
         return shard(side, group, gather_pair.at[row, step], (dp, other))
 
+    def columns_of(side):
+        return pl.ds(pl.multiple_of(side * half, half), half)
+
+    def take(side, row):
+        first = across(row)
+        blocks = wide(gathered[side, pl.ds(first * PLANE, PLANE)])
+        span = pl.ds(pl.multiple_of(first * layer_tokens, layer_tokens), layer_tokens)
+        normed[span, columns_of(side)] = narrow(blocks.reshape(layer_tokens, half))
+
     for step in range(1, layers):
         line_copy(step).start()
     for step in (3, 1, 2):
@@ -252,10 +262,10 @@
         for step in range(1, PLANE):
             pair_copy(core, row, step).wait_recv()
             pair_copy(core, row, step).start()
+        take(core, row)
 
     def half_logits(side):
-        span = pl.ds(pl.multiple_of(side * half, half), half)
-        normed[:, span] = narrow(wide(gathered[side]).reshape(tokens, half))
+        span = columns_of(side)
         return lax.dot_general(
             head[:, span],
             normed[:, span],
@@ -269,6 +279,7 @@
         for step in range(PLANE):
             if row + step > 0:
                 pair_copy(other, row, step).wait_recv()
+        take(other, row)
     logits = logits + half_logits(other)
 
     lane = lax.broadcasted_iota(jnp.int32, (1, tokens), 1)
@@ -583,12 +594,18 @@
 
 def settle_kernel(count, *refs):
     held, sems = refs[2 * count : -1], refs[-1]
-    loads = [
-        pltpu.make_async_copy(refs[i], held[i], sems.at[0, i]) for i in range(count)
-    ]
-    stores = [
-        pltpu.make_async_copy(held[i], refs[count + i], sems.at[1, i]) for i in range(count)
-    ]
+    loads, stores = [], []
+    for index in range(count):
+        rows = held[index].shape[0]
+        parts = SETTLE_PARTS if rows % (SETTLE_PARTS * 16) == 0 else 1
+        for part in range(parts):
+            span = pl.ds(part * (rows // parts), rows // parts)
+            slot = index * SETTLE_PARTS + part
+            source, middle, target = (
+                ref.at[span] for ref in (refs[index], held[index], refs[count + index])
+            )
+            loads.append(pltpu.make_async_copy(source, middle, sems.at[0, slot]))
+            stores.append(pltpu.make_async_copy(middle, target, sems.at[1, slot]))
     for load in loads:
         load.start()
     for load, store in zip(loads, stores):
@@ -607,7 +624,7 @@
         in_specs=[hbm] * count,
         out_specs=(hbm,) * count,
         scratch_shapes=[pltpu.VMEM(x.shape, x.dtype) for x in results]
-        + [pltpu.SemaphoreType.DMA((2, count))],
+        + [pltpu.SemaphoreType.DMA((2, count * SETTLE_PARTS))],
         compiler_params=pltpu.CompilerParams(vmem_limit_bytes=VMEM_BYTES),
     )(*results)
     grad_hidden, grad_gain, head_new, moment_new, second_new = settled

time: 46.6 us -> 46.6 us (level)
  no operation moved by 1% of the time
where the time goes in v3:
time: 46.6 us; the launch traced here: 46.4 us
  Pallas kernels  45.8 us (98%)
  between operations  0.64 us (1%)
    pallas_call x1, Pallas kernels, fused(): pl.pallas_call(functools.partial(fused_kernel, layers), out_shape=(jax.Sh...  43.1 us
    pallas_call x1, Pallas kernels, settle(): pl.pallas_call(functools.partial(settle_kernel, count), out_shape=tuple((...  2.67 us

profile of v3, /device:TPU:0, one launch (start us, length us, event | category | flops | bytes accessed | tf_op | source)
XLA Modules:
  0.0 46.4 jit_solution(12166969770032551038)
XLA Ops:
  0.6 43.1 %shard_map.101 = (bf16[8,4096]{1,0:T(8,128)(2,1)}, f32[32,128]{1,0:T(8,128)}, bf16[128,4096]{1,0:T(8,128)(2,1)}, bf16[128,4096]{1,0:T(8,128)(2,1)}, f32[1,128]{1,0:T(1,128)}) custom-call(bf16[8,4096]{1,0:T(8,128)(2,1)} %hidden_hbm.1, bf16[32,128]{1,0:T(8,128)(2,1)} %bitcast.4, bf16[128,4096]{1,0:T(8,128)(2,1)} %head_hbm.1, bf16[128,4096]{1,0:T(8,128)(2,1)} %moment_hbm.1, ...), custom_call_target="tpu_custom_call" | custom-call | tf_op jit(solution)/shard_map/pallas_call | solution.py:541
  43.7 2.7 %shard_map.102 = (bf16[8,4096]{1,0:T(8,128)(2,1)}, f32[32,128]{1,0:T(8,128)}, bf16[128,4096]{1,0:T(8,128)(2,1)}, bf16[128,4096]{1,0:T(8,128)(2,1)}, f32[1,128]{1,0:T(1,128)}) custom-call(bf16[8,4096]{1,0:T(8,128)(2,1)} %get-tuple-element.15.refs_0_, f32[32,128]{1,0:T(8,128)} %get-tuple-element.16.refs_1_, bf16[128,4096]{1,0:T(8,128)(2,1)} %get-tuple-element.17.refs_2_, ...), custom_call_target="tpu_custom_call" | custom-call | tf_op jit(solution)/shard_map/pallas_call | solution.py:621
